TPU v7x, 512 devices: a whole 4x4x16 slice. The times are simulated.
512 devices in a mesh: expert: 64 (over x, z), dp: 4 (over y), test: 2 (over core).
Axes of the slice: x: 4, y: 4, z: 16, core: 2. Of those that a mesh axis runs over, the one named last changes fastest.
Arguments:
- tokens: bfloat16 [16384, 3584], P(('expert', 'dp'), 'test'), may hold values from -6 to 6
- out_grad: bfloat16 [16384, 3584], P(('expert', 'dp'), 'test'), may hold values from -6 to 6
- route_ids: int32 [16384, 8], P(('expert', 'dp')), may hold values from 0 to 255, as said below
- route_slots: int32 [16384, 8], P(('expert', 'dp')), may hold values from -1 to 1, as said below
- route_weight: bfloat16 [16384, 8], P(('expert', 'dp')), may hold values from 0.19921875 to 1
- w_gate: bfloat16 [64, 3584, 1024], P('expert', None, ('dp', 'test')), may hold values from -0.09375 to 0.09375
- w_up: bfloat16 [64, 3584, 1024], P('expert', None, ('dp', 'test')), may hold values from -0.09375 to 0.09375
- w_down: bfloat16 [64, 1024, 3584], P('expert', ('dp', 'test')), may hold values from -0.1875 to 0.1875
- proj_hidden: bfloat16 [64, 64, 1024], P('expert', None, ('dp', 'test')), may hold values from -0.1875 to 0.1875
- proj_grad: bfloat16 [64, 64, 3584], P('expert'), may hold values from -0.09375 to 0.09375
- test_feats: bfloat16 [64, 256, 4096], P('expert', 'test'), may hold values from -0.09375 to 0.09375
Outputs:
- in_grad: bfloat16 [16384, 3584], P(('expert', 'dp'), 'test')
- scores: float32 [16384, 256], P(('expert', 'dp'), 'test')
Inputs may be any that keep to these rules, and one draw needn't show every extreme that they name: `route_ids`: each row names 8 different experts. `route_slots`: A route's slot is -1 exactly when its expert is 64 or more, or when 2 earlier tokens of the same aligned block of 64 rows already take that expert; otherwise it is the number of earlier tokens of that block routed to that expert.
All inputs are finite; a program needn't handle non-finite values.
Results may differ from a plain program's by a relative error of at most 0.0065.
Values may be sent and summed in bfloat16 or wider, within the bound.
A program may use at most 64 MiB of HBM per device.

v0:
```python
import jax
import jax.numpy as jnp
from jax import lax
from jax.sharding import PartitionSpec as P

CAP = 2


def pick_tables(ids_in, slots_in, weights_in, experts):
    live_mask = (slots_in >= 0) & (ids_in < experts)
    slot_code = jnp.where(live_mask, ids_in * CAP + slots_in, -1)
    columns = jnp.arange(experts * CAP, dtype=jnp.int32)
    matches = slot_code[:, :, None] == columns[None, None, :]
    picks = jnp.sum(matches.astype(jnp.float32), axis=1)
    weighted = jnp.sum(jnp.where(matches, weights_in.astype(jnp.float32)[:, :, None], 0.0), axis=1)
    return (picks, weighted)


def expert_pass(flat_in, flat_grad, gate_w, up_w, down_w, hid_proj):
    gate_pre = jnp.dot(flat_in, gate_w, preferred_element_type=jnp.float32)
    up_pre = jnp.dot(flat_in, up_w, preferred_element_type=jnp.float32)
    sigmoid_gate = jax.nn.sigmoid(gate_pre)
    act_gate = gate_pre * sigmoid_gate
    hidden = (act_gate * up_pre).astype(jnp.bfloat16)
    proj_part = lax.dot_general(
        hidden, hid_proj, (((1,), (1,)), ((), ())), preferred_element_type=jnp.float32
    )
    hid_grad = lax.dot_general(
        flat_grad, down_w, (((1,), (1,)), ((), ())), preferred_element_type=jnp.float32
    )
    up_grad = (hid_grad * act_gate).astype(jnp.bfloat16)
    gate_grad = (hid_grad * up_pre * sigmoid_gate * (1.0 + gate_pre * (1.0 - sigmoid_gate))).astype(
        jnp.bfloat16
    )
    return (proj_part, gate_grad, up_grad)


def score_rows(hidden_vec, grad_vec, test_rows):
    row_total = hidden_vec.shape[0]
    feature = (
        (hidden_vec[:, :, None] * grad_vec[:, None, :]).reshape(row_total, -1).astype(jnp.bfloat16)
    )
    return lax.dot_general(
        feature, test_rows, (((1,), (1,)), ((), ())), preferred_element_type=jnp.float32
    )


def on_device(
    tokens,
    out_grad,
    route_ids,
    route_slots,
    route_weight,
    w_gate,
    w_up,
    w_down,
    proj_hidden,
    proj_grad,
    test_feats,
):
    experts = lax.axis_size("expert")
    groups = lax.axis_size("dp")
    halves = lax.axis_size("test")
    tok_rows = tokens.shape[0]
    half_width = tokens.shape[1]
    slots_all = experts * CAP
    full_in, full_grad = (
        lax.all_gather(tokens, "test", axis=1, tiled=True),
        lax.all_gather(out_grad, "test", axis=1, tiled=True),
    )
    full_width = full_in.shape[1]
    grad_proj = proj_grad[0]
    test_rows = test_feats[0]
    own_pick, own_weight = pick_tables(route_ids, route_slots, route_weight, experts)
    all_in, all_grad, all_ids, all_slots, all_weight = (
        lax.all_gather(full_in, "dp", axis=0, tiled=True),
        lax.all_gather(full_grad, "dp", axis=0, tiled=True),
        lax.all_gather(route_ids, "dp", axis=0, tiled=True),
        lax.all_gather(route_slots, "dp", axis=0, tiled=True),
        lax.all_gather(route_weight, "dp", axis=0, tiled=True),
    )
    group_tok = all_in.shape[0]
    pick_all, weight_all = pick_tables(all_ids, all_slots, all_weight, experts)
    owner_idx = jnp.arange(group_tok, dtype=jnp.int32) // tok_rows
    in_group = (owner_idx[None, :] == jnp.arange(groups, dtype=jnp.int32)[:, None]).astype(
        jnp.float32
    )
    select = (
        (pick_all.T.reshape(experts, 1, CAP, group_tok) * in_group.reshape(1, groups, 1, group_tok))
        .reshape(-1, group_tok)
        .astype(jnp.bfloat16)
    )
    select_w = (
        (
            weight_all.T.reshape(experts, 1, CAP, group_tok)
            * in_group.reshape(1, groups, 1, group_tok)
        )
        .reshape(-1, group_tok)
        .astype(jnp.bfloat16)
    )
    in_buf = jnp.dot(select, all_in, preferred_element_type=jnp.float32).astype(jnp.bfloat16)
    grad_buf = jnp.dot(select_w, all_grad, preferred_element_type=jnp.float32).astype(jnp.bfloat16)
    rows_per = groups * CAP
    recv_in, recv_grad = (
        lax.all_to_all(
            in_buf.reshape(experts, rows_per, full_width),
            "expert",
            split_axis=0,
            concat_axis=0,
            tiled=True,
        ),
        lax.all_to_all(
            grad_buf.reshape(experts, rows_per, full_width),
            "expert",
            split_axis=0,
            concat_axis=0,
            tiled=True,
        ),
    )
    flat_in = recv_in.reshape(-1, full_width)
    flat_grad = recv_grad.reshape(-1, full_width)
    gate_w = w_gate[0]
    up_w = w_up[0]
    proj_part, gate_grad, up_grad = expert_pass(
        flat_in, flat_grad, gate_w, up_w, w_down[0], proj_hidden[0]
    )
    parts = lax.dot_general(
        gate_grad, gate_w, (((1,), (1,)), ((), ())), preferred_element_type=jnp.float32
    )
    parts = (
        parts
        + lax.dot_general(
            up_grad, up_w, (((1,), (1,)), ((), ())), preferred_element_type=jnp.float32
        )
    ).astype(jnp.bfloat16)
    hidden_vec = lax.psum(proj_part, ("dp", "test"))
    my_group = lax.axis_index("dp")
    hid_mine = lax.dynamic_index_in_dim(
        hidden_vec.reshape(experts, groups, CAP, -1), my_group, 1, keepdims=False
    ).reshape(slots_all, -1)
    grad_rows = lax.dynamic_index_in_dim(
        recv_grad.reshape(experts, groups, CAP, full_width), my_group, 1, keepdims=False
    ).reshape(slots_all, full_width)
    grad_mine = lax.dot_general(
        grad_rows, grad_proj, (((1,), (1,)), ((), ())), preferred_element_type=jnp.float32
    )
    route_score = (
        score_rows(hid_mine, grad_mine, test_rows).astype(jnp.bfloat16).reshape(experts, CAP, -1)
    )
    back_parts, back_score = (
        lax.all_to_all(
            parts.reshape(experts, rows_per, full_width),
            "expert",
            split_axis=0,
            concat_axis=0,
            tiled=True,
        ),
        lax.all_to_all(route_score, "expert", split_axis=0, concat_axis=0, tiled=True),
    )
    part_rows = back_parts.reshape(-1, full_width)
    first_row = jnp.int32(0)
    pieces = []
    for block_step in range(tok_rows * lax.axis_size(("dp", "test")) // tok_rows):
        block_idx = first_row // tok_rows + block_step
        owner_block = block_idx // halves
        half_idx = block_idx % halves
        picked_cols = lax.dynamic_slice_in_dim(select, owner_block * tok_rows, tok_rows, 1)
        part_cols = lax.dynamic_slice_in_dim(part_rows, half_idx * half_width, half_width, 1)
        pieces.append(
            lax.dot_general(
                picked_cols, part_cols, (((0,), (0,)), ((), ())), preferred_element_type=jnp.float32
            )
        )
    in_grad = lax.psum_scatter(
        jnp.concatenate(pieces, axis=0), ("dp", "test"), scatter_dimension=0, tiled=True
    ).astype(jnp.bfloat16)
    scores_out = jnp.dot(
        own_pick.astype(jnp.bfloat16),
        back_score.reshape(slots_all, -1),
        preferred_element_type=jnp.float32,
    )
    return (in_grad, scores_out)


def solution(mesh):
    placed = (
        P(("expert", "dp"), "test"),
        P(("expert", "dp"), "test"),
        P(("expert", "dp"), None),
        P(("expert", "dp"), None),
        P(("expert", "dp"), None),
        P("expert", None, ("dp", "test")),
        P("expert", None, ("dp", "test")),
        P("expert", ("dp", "test"), None),
        P("expert", None, ("dp", "test")),
        P("expert", None, None),
        P("expert", "test", None),
    )
    return jax.shard_map(
        on_device,
        mesh=mesh,
        in_specs=placed,
        out_specs=(P(("expert", "dp"), "test"), P(("expert", "dp"), "test")),
        check_vma=False,
    )
```

profile of v0, /device:TPU:4, one launch (start us, length us, event | category | flops | bytes accessed | tf_op | source)
XLA Modules:
  0.0 659.0 jit_solution(9366702021190305749)
XLA Ops:
  7.2 3.9 all_gather.26
  11.1 12.7 %all-gather = s32[4,64,8]{1,2,0:T(8,128)S(1)} all-gather(s32[1,64,8]{1,2,0:T(8,128)} %bitcast.65), channel_id=1, replica_groups=mesh['expert'=64,'dp'=4,'test'=2] {'dp'}, dimensions={0}, use_global_device_ids=true | all-gather | bytes 10240 | tf_op jit(solution)/shard_map/all_gather | solution.py:79
  23.8 12.1 %all-gather.1 = s32[4,64,8]{1,2,0:T(8,128)S(1)} all-gather(s32[1,64,8]{1,2,0:T(8,128)} %bitcast.66), channel_id=1, replica_groups=mesh['expert'=64,'dp'=4,'test'=2] {'dp'}, dimensions={0}, use_global_device_ids=true | all-gather | bytes 10240 | tf_op jit(solution)/shard_map/all_gather | solution.py:78
  36.1 10.8 %all-gather.2 = bf16[4,64,8]{1,2,0:T(8,128)(2,1)S(1)} all-gather(bf16[1,64,8]{1,2,0:T(8,128)(2,1)} %bitcast.67), channel_id=1, replica_groups=mesh['expert'=64,'dp'=4,'test'=2] {'dp'}, dimensions={0}, use_global_device_ids=true | all-gather | bytes 5120 | tf_op jit(solution)/shard_map/all_gather | solution.py:80
  46.9 0.1 copy.50
  47.0 1.5 select_reduce_fusion
  48.9 0.4 multiply_convert_fusion.1
  49.2 0.1 convert_element_type.72
  49.4 2.8 all-gather.8.cloned.1.call-done
  52.2 4.4 fusion.1
  56.6 16.3 %all-to-all-start.1 = ((bf16[64,8,3584]{2,1,0:T(8,128)(2,1)}), bf16[64,8,3584]{2,1,0:T(8,128)(2,1)}, u32[]{:S(2)}, u32[]{:S(2)}) async-start(bf16[64,8,3584]{2,1,0:T(8,128)(2,1)} %fusion.1), calls=%async_computation.1 | async-start | bytes 7340032 | tf_op jit(solution)/shard_map/all_to_all | solution.py:105
  73.0 2.3 all_gather.24
  75.3 0.1 convert_element_type.75
  75.4 37.0 %all-gather.6.cloned.1.call-done = bf16[256,3584]{1,0:T(8,128)(2,1)} async-done(((bf16[64,3584]{1,0:T(8,128)(2,1)}), bf16[256,3584]{1,0:T(8,128)(2,1)}) %all-gather.6.cloned.1.call-update) | async-done | bytes 1835024 | tf_op jit(solution)/shard_map/all_gather | solution.py:77
  112.4 4.5 fusion
  116.9 118.8 %all-to-all-done.1 = bf16[64,8,3584]{2,1,0:T(8,128)(2,1)} async-done(((bf16[64,8,3584]{2,1,0:T(8,128)(2,1)}), bf16[64,8,3584]{2,1,0:T(8,128)(2,1)}, u32[]{:S(2)}, u32[]{:S(2)}) %all-to-all-start.1) | async-done | bytes 3670048 | tf_op jit(solution)/shard_map/all_to_all | solution.py:105
  235.7 10.0 %all-to-all-start = ((bf16[64,8,3584]{2,1,0:T(8,128)(2,1)}), bf16[64,8,3584]{2,1,0:T(8,128)(2,1)}, u32[]{:S(2)}, u32[]{:S(2)}) async-start(bf16[64,8,3584]{2,1,0:T(8,128)(2,1)} %fusion), calls=%async_computation | async-start | bytes 7340032 | tf_op jit(solution)/shard_map/all_to_all | solution.py:112
  245.7 3.2 fusion.3
  249.0 3.8 fusion.5
  252.8 155.7 %all-to-all-done = bf16[64,8,3584]{2,1,0:T(8,128)(2,1)} async-done(((bf16[64,8,3584]{2,1,0:T(8,128)(2,1)}), bf16[64,8,3584]{2,1,0:T(8,128)(2,1)}, u32[]{:S(2)}, u32[]{:S(2)}) %all-to-all-start) | async-done | bytes 3670048 | tf_op jit(solution)/shard_map/all_to_all | solution.py:112
  408.5 3.4 fusion.7
  412.0 1.1 fusion.18
  413.1 3.0 fusion.2
  416.2 10.1 %all-to-all-start.2 = ((bf16[64,8,3584]{2,1,0:T(8,128)(2,1)}), bf16[64,8,3584]{2,1,0:T(8,128)(2,1)}, u32[]{:S(2)}, u32[]{:S(2)}) async-start(bf16[64,8,3584]{2,1,0:T(8,128)(2,1)} %fusion.2), calls=%async_computation.2 | async-start | bytes 7340032 | tf_op jit(solution)/shard_map/all_to_all | solution.py:151
  426.4 0.9 fusion.27
  427.3 0.2 reduce-scatter.2.cloned.1.call-start
  427.6 161.6 %all-to-all-done.2 = bf16[64,8,3584]{2,1,0:T(8,128)(2,1)} async-done(((bf16[64,8,3584]{2,1,0:T(8,128)(2,1)}), bf16[64,8,3584]{2,1,0:T(8,128)(2,1)}, u32[]{:S(2)}, u32[]{:S(2)}) %all-to-all-start.2) | async-done | bytes 3670048 | tf_op jit(solution)/shard_map/all_to_all | solution.py:151
  589.2 2.7 convolution_dynamic-update-slice_fusion.7
  591.9 2.8 convolution_dynamic-update-slice_fusion.6
  594.7 2.8 convolution_dynamic-update-slice_fusion.5
  597.5 2.9 convolution_dynamic-update-slice_fusion.4
  600.4 2.7 convolution_dynamic-update-slice_fusion.3
  603.1 2.7 convolution_dynamic-update-slice_fusion.2
  605.8 2.8 convolution_dynamic-update-slice_fusion.1
  608.7 2.8 convolution_dynamic-update-slice_fusion
  611.5 8.1 %reshape.114 = bf16[64,4,2,3584]{3,2,1,0:T(2,128)(2,1)} reshape(bf16[64,8,3584]{2,1,0:T(8,128)(2,1)} %all-to-all-done) | data formatting | bytes 7340032 | tf_op jit(solution)/shard_map/reshape | solution.py:142
  619.6 1.9 constant_dynamic-slice_fusion
  621.5 0.3 reshape.115
  621.9 0.4 fusion.24
  622.3 0.9 constant_dynamic-slice_fusion.1
  623.3 0.3 multiply_convert_fusion
  623.6 1.1 convolution_convert_fusion.2
  624.7 9.9 %all-to-all-start.3 = ((bf16[64,2,128]{2,1,0:T(2,128)(2,1)}), bf16[64,2,128]{2,1,0:T(2,128)(2,1)S(1)}, u32[]{:S(2)}, u32[]{:S(2)}) async-start(bf16[64,2,128]{2,1,0:T(2,128)(2,1)} %bitcast.22), calls=%async_computation.4 | async-start | bytes 65536 | tf_op jit(solution)/shard_map/all_to_all | solution.py:158
  634.7 0.2 convert_reduce_fusion.1
  634.8 12.4 %all-to-all-done.3 = bf16[64,2,128]{2,1,0:T(2,128)(2,1)S(1)} async-done(((bf16[64,2,128]{2,1,0:T(2,128)(2,1)}), bf16[64,2,128]{2,1,0:T(2,128)(2,1)S(1)}, u32[]{:S(2)}, u32[]{:S(2)}) %all-to-all-start.3) | async-done | bytes 32800 | tf_op jit(solution)/shard_map/all_to_all | solution.py:158
  647.2 0.7 fusion.46
  648.0 2.8 reduce-scatter.2.cloned.1.call-done
  650.7 1.7 convert_element_type.81
  (39 shorter events, 0.9 us)
Async XLA Ops:
  7.2 616.4 %copy-start = (bf16[1,128,4096]{2,1,0:T(8,128)(2,1)S(1)}, bf16[1,128,4096]{2,1,0:T(8,128)(2,1)}, u32[]{:S(2)}) copy-start(bf16[1,128,4096]{2,1,0:T(8,128)(2,1)} %param.21) | copy-start | bytes 3145732
  7.2 45.0 %all-gather.8.cloned.1.call-start = ((), (), s32[]{:S(2)}) async-start(), calls=%async_computation.6 | async-start | bytes 2293760 | tf_op jit(solution)/shard_map/all_gather | solution.py:76
  56.6 16.4 %copy-start.6 = (bf16[64,1792]{1,0:T(8,128)(2,1)S(1)}, bf16[64,1792]{1,0:T(8,128)(2,1)}, u32[]{:S(2)}) copy-start(bf16[64,1792]{1,0:T(8,128)(2,1)} %param.12) | copy-start | bytes 688132
  56.6 179.1 %all-to-all-start.1 = ((bf16[64,8,3584]{2,1,0:T(8,128)(2,1)}), bf16[64,8,3584]{2,1,0:T(8,128)(2,1)}, u32[]{:S(2)}, u32[]{:S(2)}) async-start(bf16[64,8,3584]{2,1,0:T(8,128)(2,1)} %fusion.1), calls=%async_computation.1 | async-start | bytes 7340032 | tf_op jit(solution)/shard_map/all_to_all | solution.py:105
  72.9 39.5 %all-gather.6.cloned.1.call-start = ((), (), s32[]{:S(2)}) async-start(), calls=%async_computation.5 | async-start | bytes 2293760 | tf_op jit(solution)/shard_map/all_gather | solution.py:77
  116.9 128.8 %copy-start.1 = (bf16[1,3584,128]{2,1,0:T(8,128)(2,1)S(1)}, bf16[1,3584,128]{2,1,0:T(8,128)(2,1)}, u32[]{:S(2)}) copy-start(bf16[1,3584,128]{2,1,0:T(8,128)(2,1)} %param.16) | copy-start | bytes 2752516
  235.7 172.8 %all-to-all-start = ((bf16[64,8,3584]{2,1,0:T(8,128)(2,1)}), bf16[64,8,3584]{2,1,0:T(8,128)(2,1)}, u32[]{:S(2)}, u32[]{:S(2)}) async-start(bf16[64,8,3584]{2,1,0:T(8,128)(2,1)} %fusion), calls=%async_computation | async-start | bytes 7340032 | tf_op jit(solution)/shard_map/all_to_all | solution.py:112
  245.7 3.2 copy-start.2
  408.5 3.4 copy-start.3
  416.2 10.2 %copy-start.4 = (f32[512,128]{1,0:T(8,128)S(1)}, f32[512,128]{1,0:T(8,128)}, u32[]{:S(2)}) copy-start(f32[512,128]{1,0:T(8,128)} %fusion.5) | copy-start | bytes 786436
  416.2 10.2 %copy-start.9 = (bf16[1,64,128]{2,1,0:T(8,128)(2,1)S(1)}, bf16[1,64,128]{2,1,0:T(8,128)(2,1)}, u32[]{:S(2)}) copy-start(bf16[1,64,128]{2,1,0:T(8,128)(2,1)} %param.19) | copy-start | bytes 49156
  416.2 173.0 %all-to-all-start.2 = ((bf16[64,8,3584]{2,1,0:T(8,128)(2,1)}), bf16[64,8,3584]{2,1,0:T(8,128)(2,1)}, u32[]{:S(2)}, u32[]{:S(2)}) async-start(bf16[64,8,3584]{2,1,0:T(8,128)(2,1)} %fusion.2), calls=%async_computation.2 | async-start | bytes 7340032 | tf_op jit(solution)/shard_map/all_to_all | solution.py:151
  426.3 196.0 %all-reduce.2.cloned.1.call-start = ((), (), s32[]{:S(2)}) async-start(), calls=%async_computation.8 | async-start | bytes 524288 | tf_op jit(solution)/shard_map/psum | solution.py:136
  427.3 223.4 %reduce-scatter.2.cloned.1.call-start = ((), (), s32[]{:S(2)}) async-start(), calls=%async_computation.7 | async-start | bytes 4128768 | tf_op jit(solution)/shard_map/reduce_scatter | solution.py:174
  619.6 2.2 copy-start.5
  621.5 13.0 %copy-start.7 = (s32[64,8]{0,1:T(8,128)S(1)}, s32[64,8]{0,1:T(8,128)}, u32[]{:S(2)}) copy-start(s32[64,8]{0,1:T(8,128)} %param.14) | copy-start | bytes 6148
  621.5 13.0 %copy-start.8 = (s32[64,8]{0,1:T(8,128)S(1)}, s32[64,8]{0,1:T(8,128)}, u32[]{:S(2)}) copy-start(s32[64,8]{0,1:T(8,128)} %param.13) | copy-start | bytes 6148
  624.7 22.5 %all-to-all-start.3 = ((bf16[64,2,128]{2,1,0:T(2,128)(2,1)}), bf16[64,2,128]{2,1,0:T(2,128)(2,1)S(1)}, u32[]{:S(2)}, u32[]{:S(2)}) async-start(bf16[64,2,128]{2,1,0:T(2,128)(2,1)} %bitcast.22), calls=%async_computation.4 | async-start | bytes 65536 | tf_op jit(solution)/shard_map/all_to_all | solution.py:158
Sparse Core Ops, SparseCore 0:
  11.3 40.8 all-gather.7
  75.9 36.4 all-gather.5
  429.5 76.6 all-reduce.1
  611.6 39.0 reduce-scatter.1
where the time goes:
time: 660 us; the launch traced here: 659 us
  waiting for transfers between devices  491 us (74%)
  matrix products  49.1 us (7%)
  starting transfers between devices  46.7 us (7%)
  blocking collectives  41.8 us (6%)
  between operations  14.1 us (2%)
  local copies, waits for them, and re-layouts  12.1 us (2%)
    all_to_all x1, waiting for transfers between devices, on_device(): lax.all_to_all(parts.reshape(experts, rows_per, full_width), 'expert', sp...  162 us
    all_to_all x1, waiting for transfers between devices, on_device(): lax.all_to_all(grad_buf.reshape(experts, rows_per, full_width), 'expert',...  156 us
    all_to_all x1, waiting for transfers between devices, on_device(): lax.all_to_all(in_buf.reshape(experts, rows_per, full_width), 'expert', s...  119 us
    all_gather x1, waiting for transfers between devices, on_device(): lax.all_gather(full_grad, 'dp', axis=0, tiled=True)  37 us
    dot_general x8, matrix products, on_device(): lax.dot_general(picked_cols, part_cols, (((0,), (0,)), ((), ())), preferr...  22.3 us
    all_to_all x1, starting transfers between devices, on_device(): lax.all_to_all(in_buf.reshape(experts, rows_per, full_width), 'expert', s...  16.3 us
  transfers between devices with their start and end apart: 8, of which 7 were waited for; matrix products, arithmetic and copies ran while one was open for 8% of the time, Pallas kernels for 0%

commit v1 on v0

--- a/solution.py
+++ b/solution.py
@@ -4,6 +4,13 @@
 from jax.sharding import PartitionSpec as P
 
 CAP = 2
+
+
+def all_by_exchange(array, axis, dim):
+    n_dev = lax.axis_size(axis)
+    blocks = jnp.stack([array for _ in range(n_dev)])
+    blocks = lax.all_to_all(blocks, axis, split_axis=0, concat_axis=0)
+    return jnp.concatenate(blocks, axis=dim)
 
 
 def pick_tables(ids_in, slots_in, weights_in, experts):
@@ -74,7 +81,7 @@
     own_pick, own_weight = pick_tables(route_ids, route_slots, route_weight, experts)
     all_in, all_grad, all_ids, all_slots, all_weight = (
         lax.all_gather(full_in, "dp", axis=0, tiled=True),
-        lax.all_gather(full_grad, "dp", axis=0, tiled=True),
+        all_by_exchange(full_grad, "dp", 0),
         lax.all_gather(route_ids, "dp", axis=0, tiled=True),
         lax.all_gather(route_slots, "dp", axis=0, tiled=True),
         lax.all_gather(route_weight, "dp", axis=0, tiled=True),

time: 660 us -> 667 us (1.011)
  the two profiles are of different devices: /device:TPU:4 before, /device:TPU:2 now
where the time goes in v1:
time: 667 us; the launch traced here: 666 us
  waiting for transfers between devices  473 us (71%)
  blocking collectives  56.1 us (8%)
  starting transfers between devices  54.4 us (8%)
  matrix products  47.8 us (7%)
  local copies, waits for them, and re-layouts  15.2 us (2%)
  between operations  14.1 us (2%)
    all_to_all x1, waiting for transfers between devices, on_device(): lax.all_to_all(parts.reshape(experts, rows_per, full_width), 'expert', sp...  158 us
    all_to_all x1, waiting for transfers between devices, on_device(): lax.all_to_all(in_buf.reshape(experts, rows_per, full_width), 'expert', s...  153 us
    all_to_all x1, waiting for transfers between devices, on_device(): lax.all_to_all(grad_buf.reshape(experts, rows_per, full_width), 'expert',...  111 us
    all_gather x1, waiting for transfers between devices, on_device(): lax.all_gather(full_in, 'dp', axis=0, tiled=True)  37 us
    all_gather x1, blocking collectives, on_device(): lax.all_gather(route_slots, 'dp', axis=0, tiled=True)  28.9 us
    dot_general x8, matrix products, on_device(): lax.dot_general(picked_cols, part_cols, (((0,), (0,)), ((), ())), preferr...  22.4 us
    all_to_all x1, starting transfers between devices, on_device(): lax.all_to_all(grad_buf.reshape(experts, rows_per, full_width), 'expert',...  18.9 us
  transfers between devices with their start and end apart: 8, of which 6 were waited for; matrix products, arithmetic and copies ran while one was open for 8% of the time, Pallas kernels for 0%

profile of v1, /device:TPU:2, one launch (start us, length us, event | category | flops | bytes accessed | tf_op | source)
XLA Modules:
  0.0 665.5 jit_solution(14494402430547614668)
XLA Ops:
  7.2 2.5 all_gather.21
  9.7 1.4 stack.2
  11.1 4.5 all-to-all-start
  15.6 28.9 %all-gather = s32[4,64,8]{1,2,0:T(8,128)S(1)} all-gather(s32[1,64,8]{1,2,0:T(8,128)S(1)} %bitcast.67), channel_id=1, replica_groups=mesh['expert'=64,'dp'=4,'test'=2] {'dp'}, dimensions={0}, use_global_device_ids=true | all-gather | bytes 10240 | tf_op jit(solution)/shard_map/all_gather | solution.py:86
  44.5 12.0 %all-gather.1 = s32[4,64,8]{1,2,0:T(8,128)S(1)} all-gather(s32[1,64,8]{1,2,0:T(8,128)S(1)} %bitcast.68), channel_id=1, replica_groups=mesh['expert'=64,'dp'=4,'test'=2] {'dp'}, dimensions={0}, use_global_device_ids=true | all-gather | bytes 10240 | tf_op jit(solution)/shard_map/all_gather | solution.py:85
  56.6 10.4 %all-gather.2 = bf16[4,64,8]{1,2,0:T(8,128)(2,1)S(1)} all-gather(bf16[1,64,8]{1,2,0:T(8,128)(2,1)S(1)} %bitcast.69), channel_id=1, replica_groups=mesh['expert'=64,'dp'=4,'test'=2] {'dp'}, dimensions={0}, use_global_device_ids=true | all-gather | bytes 5120 | tf_op jit(solution)/shard_map/all_gather | solution.py:87
  67.2 1.5 select_reduce_fusion
  69.1 1.1 multiply_convert_fusion.1
  70.2 1.1 convert_element_type.81
  71.2 3.0 fusion
  74.2 18.9 %all-to-all-start.1 = ((bf16[64,8,3584]{2,1,0:T(8,128)(2,1)}), bf16[64,8,3584]{2,1,0:T(8,128)(2,1)}, u32[]{:S(2)}, u32[]{:S(2)}) async-start(bf16[64,8,3584]{2,1,0:T(8,128)(2,1)} %fusion), calls=%async_computation.1 | async-start | bytes 7340032 | tf_op jit(solution)/shard_map/all_to_all | solution.py:119
  93.2 2.3 all_gather.22
  95.6 37.0 %all-gather.5.cloned.1.call-done = bf16[256,3584]{1,0:T(8,128)(2,1)} async-done(((bf16[64,3584]{1,0:T(8,128)(2,1)}), bf16[256,3584]{1,0:T(8,128)(2,1)}) %all-gather.5.cloned.1.call-update) | async-done | bytes 1835024 | tf_op jit(solution)/shard_map/all_gather | solution.py:83
  132.6 4.5 fusion.1
  137.1 110.9 %all-to-all-done.1 = bf16[64,8,3584]{2,1,0:T(8,128)(2,1)} async-done(((bf16[64,8,3584]{2,1,0:T(8,128)(2,1)}), bf16[64,8,3584]{2,1,0:T(8,128)(2,1)}, u32[]{:S(2)}, u32[]{:S(2)}) %all-to-all-start.1) | async-done | bytes 3670048 | tf_op jit(solution)/shard_map/all_to_all | solution.py:119
  248.1 10.4 %all-to-all-start.2 = ((bf16[64,8,3584]{2,1,0:T(8,128)(2,1)}), bf16[64,8,3584]{2,1,0:T(8,128)(2,1)}, u32[]{:S(2)}, u32[]{:S(2)}) async-start(bf16[64,8,3584]{2,1,0:T(8,128)(2,1)} %fusion.1), calls=%async_computation.2 | async-start | bytes 7340032 | tf_op jit(solution)/shard_map/all_to_all | solution.py:112
  258.5 4.2 fusion.7
  262.7 152.5 %all-to-all-done.2 = bf16[64,8,3584]{2,1,0:T(8,128)(2,1)} async-done(((bf16[64,8,3584]{2,1,0:T(8,128)(2,1)}), bf16[64,8,3584]{2,1,0:T(8,128)(2,1)}, u32[]{:S(2)}, u32[]{:S(2)}) %all-to-all-start.2) | async-done | bytes 3670048 | tf_op jit(solution)/shard_map/all_to_all | solution.py:112
  415.2 3.2 fusion.3
  418.5 3.1 fusion.5
  421.6 0.7 copy-done.4
  422.3 1.1 fusion.18
  423.4 3.1 fusion.2
  426.5 10.7 %all-to-all-start.3 = ((bf16[64,8,3584]{2,1,0:T(8,128)(2,1)}), bf16[64,8,3584]{2,1,0:T(8,128)(2,1)}, u32[]{:S(2)}, u32[]{:S(2)}) async-start(bf16[64,8,3584]{2,1,0:T(8,128)(2,1)} %fusion.2), calls=%async_computation.3 | async-start | bytes 7340032 | tf_op jit(solution)/shard_map/all_to_all | solution.py:158
  437.2 0.9 fusion.27
  438.2 0.2 reduce-scatter.2.cloned.1.call-start
  438.4 158.4 %all-to-all-done.3 = bf16[64,8,3584]{2,1,0:T(8,128)(2,1)} async-done(((bf16[64,8,3584]{2,1,0:T(8,128)(2,1)}), bf16[64,8,3584]{2,1,0:T(8,128)(2,1)}, u32[]{:S(2)}, u32[]{:S(2)}) %all-to-all-start.3) | async-done | bytes 3670048 | tf_op jit(solution)/shard_map/all_to_all | solution.py:158
  596.8 2.7 convolution_dynamic-update-slice_fusion.7
  599.5 2.8 convolution_dynamic-update-slice_fusion.6
  602.3 2.8 convolution_dynamic-update-slice_fusion.5
  605.2 2.9 convolution_dynamic-update-slice_fusion.4
  608.0 2.7 convolution_dynamic-update-slice_fusion.3
  610.8 2.7 convolution_dynamic-update-slice_fusion.2
  613.5 2.9 convolution_dynamic-update-slice_fusion.1
  616.3 2.8 convolution_dynamic-update-slice_fusion
  619.2 8.1 %reshape.128 = bf16[64,4,2,3584]{3,2,1,0:T(2,128)(2,1)} reshape(bf16[64,8,3584]{2,1,0:T(8,128)(2,1)} %all-to-all-done.1) | data formatting | bytes 7340032 | tf_op jit(solution)/shard_map/reshape | solution.py:149
  627.3 1.9 constant_dynamic-slice_fusion
  629.2 0.3 reshape.129
  629.5 0.4 fusion.24
  630.0 0.9 constant_dynamic-slice_fusion.1
  630.9 0.3 multiply_convert_fusion
  631.2 1.1 convolution_convert_fusion.2
  632.3 9.6 %all-to-all-start.4 = ((bf16[64,2,128]{2,1,0:T(2,128)(2,1)}), bf16[64,2,128]{2,1,0:T(2,128)(2,1)S(1)}, u32[]{:S(2)}, u32[]{:S(2)}) async-start(bf16[64,2,128]{2,1,0:T(2,128)(2,1)} %bitcast.23), calls=%async_computation.5 | async-start | bytes 65536 | tf_op jit(solution)/shard_map/all_to_all | solution.py:165
  642.1 0.2 convert_reduce_fusion.1
  642.2 13.2 %all-to-all-done.4 = bf16[64,2,128]{2,1,0:T(2,128)(2,1)S(1)} async-done(((bf16[64,2,128]{2,1,0:T(2,128)(2,1)}), bf16[64,2,128]{2,1,0:T(2,128)(2,1)S(1)}, u32[]{:S(2)}, u32[]{:S(2)}) %all-to-all-start.4) | async-done | bytes 32800 | tf_op jit(solution)/shard_map/all_to_all | solution.py:165
  655.4 0.7 fusion.46
  656.2 1.0 reduce-scatter.2.cloned.1.call-done
  657.2 1.7 convert_element_type.87
  (43 shorter events, 1.0 us)
Async XLA Ops:
  7.2 624.1 %copy-start = (bf16[1,128,4096]{2,1,0:T(8,128)(2,1)S(1)}, bf16[1,128,4096]{2,1,0:T(8,128)(2,1)}, u32[]{:S(2)}) copy-start(bf16[1,128,4096]{2,1,0:T(8,128)(2,1)} %param.21) | copy-start | bytes 3145732
  7.2 8.4 %copy-start.8 = (s32[64,8]{0,1:T(8,128)S(1)}, s32[64,8]{0,1:T(8,128)}, u32[]{:S(2)}) copy-start(s32[64,8]{0,1:T(8,128)} %param.14) | copy-start | bytes 6148
  7.2 37.3 %copy-start.9 = (s32[64,8]{0,1:T(8,128)S(1)}, s32[64,8]{0,1:T(8,128)}, u32[]{:S(2)}) copy-start(s32[64,8]{0,1:T(8,128)} %param.13) | copy-start | bytes 6148
  7.2 49.4 %copy-start.10 = (bf16[64,8]{0,1:T(8,128)(2,1)S(1)}, bf16[64,8]{0,1:T(8,128)(2,1)}, u32[]{:S(2)}) copy-start(bf16[64,8]{0,1:T(8,128)(2,1)} %param.15) | copy-start | bytes 3076
  11.1 60.1 %all-to-all-start = ((bf16[4,64,3584]{2,1,0:T(8,128)(2,1)}), bf16[4,64,3584]{2,1,0:T(8,128)(2,1)S(1)}, u32[]{:S(2)}, u32[]{:S(2)}) async-start(bf16[4,64,3584]{2,1,0:T(8,128)(2,1)} %stack.2), calls=%async_computation | async-start | bytes 3670016 | tf_op jit(solution)/shard_map/all_to_all | solution.py:12
  74.2 19.0 %copy-start.7 = (bf16[64,1792]{1,0:T(8,128)(2,1)S(1)}, bf16[64,1792]{1,0:T(8,128)(2,1)}, u32[]{:S(2)}) copy-start(bf16[64,1792]{1,0:T(8,128)(2,1)} %param.11) | copy-start | bytes 688132
  74.2 173.9 %all-to-all-start.1 = ((bf16[64,8,3584]{2,1,0:T(8,128)(2,1)}), bf16[64,8,3584]{2,1,0:T(8,128)(2,1)}, u32[]{:S(2)}, u32[]{:S(2)}) async-start(bf16[64,8,3584]{2,1,0:T(8,128)(2,1)} %fusion), calls=%async_computation.1 | async-start | bytes 7340032 | tf_op jit(solution)/shard_map/all_to_all | solution.py:119
  93.2 39.4 %all-gather.5.cloned.1.call-start = ((), (), s32[]{:S(2)}) async-start(), calls=%async_computation.6 | async-start | bytes 2293760 | tf_op jit(solution)/shard_map/all_gather | solution.py:83
  248.1 167.2 %all-to-all-start.2 = ((bf16[64,8,3584]{2,1,0:T(8,128)(2,1)}), bf16[64,8,3584]{2,1,0:T(8,128)(2,1)}, u32[]{:S(2)}, u32[]{:S(2)}) async-start(bf16[64,8,3584]{2,1,0:T(8,128)(2,1)} %fusion.1), calls=%async_computation.2 | async-start | bytes 7340032 | tf_op jit(solution)/shard_map/all_to_all | solution.py:112
  258.5 156.8 %copy-start.1 = (bf16[1,3584,128]{2,1,0:T(8,128)(2,1)S(1)}, bf16[1,3584,128]{2,1,0:T(8,128)(2,1)}, u32[]{:S(2)}) copy-start(bf16[1,3584,128]{2,1,0:T(8,128)(2,1)} %param.16) | copy-start | bytes 2752516
  258.5 160.0 %copy-start.2 = (bf16[1,3584,128]{2,1,0:T(8,128)(2,1)S(1)}, bf16[1,3584,128]{2,1,0:T(8,128)(2,1)}, u32[]{:S(2)}) copy-start(bf16[1,3584,128]{2,1,0:T(8,128)(2,1)} %param.17) | copy-start | bytes 2752516
  415.2 7.0 %copy-start.3 = (f32[512,128]{1,0:T(8,128)S(1)}, f32[512,128]{1,0:T(8,128)}, u32[]{:S(2)}) copy-start(f32[512,128]{1,0:T(8,128)} %fusion.7) | copy-start | bytes 786436
  421.6 0.7 copy-start.4
  426.5 10.7 %copy-start.5 = (f32[512,128]{1,0:T(8,128)S(1)}, f32[512,128]{1,0:T(8,128)}, u32[]{:S(2)}) copy-start(f32[512,128]{1,0:T(8,128)} %copy-done.4) | copy-start | bytes 786436
  426.5 10.7 %copy-start.11 = (bf16[1,64,128]{2,1,0:T(8,128)(2,1)S(1)}, bf16[1,64,128]{2,1,0:T(8,128)(2,1)}, u32[]{:S(2)}) copy-start(bf16[1,64,128]{2,1,0:T(8,128)(2,1)} %param.19) | copy-start | bytes 49156
  426.5 170.3 %all-to-all-start.3 = ((bf16[64,8,3584]{2,1,0:T(8,128)(2,1)}), bf16[64,8,3584]{2,1,0:T(8,128)(2,1)}, u32[]{:S(2)}, u32[]{:S(2)}) async-start(bf16[64,8,3584]{2,1,0:T(8,128)(2,1)} %fusion.2), calls=%async_computation.3 | async-start | bytes 7340032 | tf_op jit(solution)/shard_map/all_to_all | solution.py:158
  437.2 192.8 %all-reduce.2.cloned.1.call-start = ((), (), s32[]{:S(2)}) async-start(), calls=%async_computation.8 | async-start | bytes 524288 | tf_op jit(solution)/shard_map/psum | solution.py:143
  438.2 219.1 %reduce-scatter.2.cloned.1.call-start = ((), (), s32[]{:S(2)}) async-start(), calls=%async_computation.7 | async-start | bytes 4128768 | tf_op jit(solution)/shard_map/reduce_scatter | solution.py:181
  627.3 2.2 copy-start.6
  632.3 23.1 %all-to-all-start.4 = ((bf16[64,2,128]{2,1,0:T(2,128)(2,1)}), bf16[64,2,128]{2,1,0:T(2,128)(2,1)S(1)}, u32[]{:S(2)}, u32[]{:S(2)}) async-start(bf16[64,2,128]{2,1,0:T(2,128)(2,1)} %bitcast.23), calls=%async_computation.5 | async-start | bytes 65536 | tf_op jit(solution)/shard_map/all_to_all | solution.py:165
Sparse Core Ops, SparseCore 0:
  96.1 36.4 all-gather.4
  440.3 76.4 all-reduce.1
  619.3 37.8 reduce-scatter.1
